TPU v7x, 32 devices: a whole 2x2x4 slice. The times are simulated.
32 devices in a mesh: mp: 8 (over z, y), dp: 4 (over x, core).
Axes of the slice: x: 2, y: 2, z: 4, core: 2. Of those that a mesh axis runs over, the one named last changes fastest.
Arguments:
- forward_fields: bfloat16 [16, 4, 16384], P(None, None, 'mp'), may hold values from -6 to 6
- adjoint_fields: bfloat16 [64, 4, 16384], P(None, None, 'mp'), may hold values from -6 to 6
- data_rec: int32 [768], P('dp'), may hold values from 0 to 63
- data_freq: int32 [768], P('dp'), may hold values from 0 to 15
- data_coef: float32 [768, 4], P('dp'), may hold values from -6 to 6
- residual_cols: bfloat16 [768, 256], P('dp'), may hold values from -6 to 6
Outputs:
- data_update: bfloat16 [768, 256], P('dp')
- model_update: float32 [16384, 256], P(('mp', 'dp'))
All inputs are finite; a program needn't handle non-finite values.
Results may differ from a plain program's by a relative error of at most 0.0075.
Values may be sent and summed in bfloat16 or wider, within the bound.
A program may use at most 64 MiB of HBM per device.

v0:
```python
import math
import jax
import jax.numpy as jnp
from jax import lax
from jax.sharding import PartitionSpec as P

GRID_COLS = 128
SWEEPS = 2


def with_halo(array, sides, width):
    for axis, dim in sides:
        peers, length = (lax.axis_size(axis), array.shape[dim])
        up = [(i, (i + 1) % peers) for i in range(peers - 1)]
        down = [(j, i) for i, j in up]
        last = lax.slice_in_dim(array, length - width, length, axis=dim)
        leading = lax.slice_in_dim(array, 0, width, axis=dim)
        before = lax.ppermute(last, axis, up)
        after = lax.ppermute(leading, axis, down)
        array = jnp.concatenate([before, array, after], axis=dim)
    return array


def sweep_once(field):
    center = field[:, 1:-1, :]
    sides = jnp.pad(center, ((0, 0), (0, 0), (1, 1)))
    beside_all = field[:, :-2, :] + field[:, 2:, :] + sides[:, :, :-2] + sides[:, :, 2:]
    return center + 0.2 * (beside_all - 4.0 * center)


def per_device(forward_fields, adjoint_fields, data_rec, data_freq, data_coef, residual_cols):
    rows_here = data_rec.shape[0]
    cells_here = forward_fields.shape[2]
    slab_rows = cells_here // GRID_COLS
    slab_count = lax.axis_size("mp")
    block_count = lax.axis_size("dp")
    adjoint = adjoint_fields[data_rec].astype(jnp.float32)
    forward = forward_fields[data_freq].astype(jnp.float32)
    sens = (0.5 * jnp.sum(data_coef[:, :, None] * adjoint * forward, axis=1)).astype(jnp.bfloat16)
    grid = sens.astype(jnp.float32).reshape(rows_here, slab_rows, GRID_COLS)
    extended = with_halo(grid.astype(jnp.bfloat16), (("mp", 1),), SWEEPS).astype(grid.dtype)
    first_row = lax.axis_index("mp") * slab_rows
    total_rows = slab_rows * slab_count
    for sweep in range(SWEEPS):
        extended = sweep_once(extended)
        margin = SWEEPS - 1 - sweep
        if margin > 0:
            global_rows = first_row - margin + jnp.arange(slab_rows + 2 * margin, dtype=jnp.int32)
            inside = (global_rows >= 0) & (global_rows < total_rows)
            extended = jnp.where(inside[None, :, None], extended, 0.0)
    grid = extended
    smooth = grid.reshape(rows_here, cells_here).astype(jnp.bfloat16)
    residual_whole = lax.all_gather(residual_cols, "dp", axis=0, tiled=True)
    gram_tile = lax.dot_general(
        smooth,
        lax.all_gather(sens, "dp", axis=0, tiled=True),
        (((1,), (1,)), ((), ())),
        preferred_element_type=jnp.float32,
    )
    partial_value = jnp.dot(
        gram_tile, residual_whole.astype(jnp.float32), precision=lax.Precision.HIGHEST
    )
    gram_prod = lax.psum(partial_value, "mp") / (cells_here * slab_count)
    data_update = (gram_prod + residual_cols.astype(jnp.float32)).astype(jnp.bfloat16)
    summed = lax.psum_scatter(
        lax.dot_general(
            smooth, data_update, (((0,), (0,)), ((), ())), preferred_element_type=jnp.float32
        ),
        "dp",
        scatter_dimension=0,
        tiled=True,
    )
    model_update = summed / math.sqrt(rows_here * block_count)
    return (data_update, model_update)


def solution(mesh):
    in_specs = (
        P(None, None, "mp"),
        P(None, None, "mp"),
        P("dp"),
        P("dp"),
        P("dp", None),
        P("dp", None),
    )
    out_specs = (P("dp", None), P(("mp", "dp"), None))
    return jax.shard_map(
        per_device, mesh=mesh, in_specs=in_specs, out_specs=out_specs, check_vma=False
    )
```

profile of v0, /device:TPU:0, one launch (start us, length us, event | category | flops | bytes accessed | tf_op | source)
XLA Modules:
  0.0 189.3 jit_solution(5085543405692865950)
XLA Ops:
  7.2 0.0 copy-start
  7.2 0.0 all-gather.2.cloned.1.call-start
  7.2 0.8 compare_select_fusion.1
  8.0 0.7 compare_select_fusion
  8.7 0.8 copy.10
  9.5 0.0 copy-done
  9.5 0.0 copy-start.1
  9.5 9.6 %gather_fusion = bf16[192,4,2048]{2,1,0:T(4,128)(2,1)} fusion(bf16[64,4,2048]{2,1,0:T(4,128)(2,1)S(1)} %copy-done, s32[1024]{0:T(1024)S(1)} %pad_clamp_fusion.1), kind=kCustom, calls=%fused_computation | custom fusion | bytes 6292224 | tf_op jit(solution)/shard_map/gather | solution.py:37
  19.1 0.0 copy-done.1
  19.1 9.7 %gather_fusion.1 = bf16[192,4,2048]{2,1,0:T(4,128)(2,1)} fusion(bf16[16,4,2048]{2,1,0:T(4,128)(2,1)S(1)} %copy-done.1, s32[1024]{0:T(1024)S(1)} %pad_clamp_fusion), kind=kCustom, calls=%fused_computation.1 | custom fusion | bytes 6292224 | tf_op jit(solution)/shard_map/gather | solution.py:38
  28.8 9.7 %multiply_reduce_fusion = f32[192,2048]{1,0:T(8,128)S(1)} fusion(bf16[192,4,2048]{2,1,0:T(4,128)(2,1)} %gather_fusion.1, bf16[192,4,2048]{2,1,0:T(4,128)(2,1)} %gather_fusion, f32[192,4]{1,0:T(8,128)S(1)} %copy.10), kind=kLoop, calls=%fused_computation.2 | loop fusion | flops 7471104 | bytes 7867392 | tf_op jit(solution)/shard_map/reduce_sum | solution.py:39
  38.5 0.0 copy-start.3
  38.5 1.0 multiply_convert_fusion
  39.5 0.0 all-gather.2.cloned.1.call-update
  39.5 0.0 all-reduce.4.cloned.1.call-start
  39.6 1.4 copy.14
  41.0 4.9 %collective-permute-start = (bf16[192,2,128]{0,2,1:T(8,128)(2,1)S(1)}, bf16[192,2,128]{0,2,1:T(8,128)(2,1)S(1)}, u32[]{:S(2)}, u32[]{:S(2)}) collective-permute-start(bf16[192,2,128]{0,2,1:T(8,128)(2,1)S(1)} %get-tuple-element.2), channel_id=1, source_target_pairs={{0,4},{4,8},{8,12},{12,16},{16,20},{20,24},{24,28},{1,5},{5,9},{9,... | collective-permute-start | bytes 294920 | tf_op jit(solution)/shard_map/ppermute | solution.py:18
  46.0 1.3 collective-permute-start.1
  47.3 0.0 copy-done.3
  47.3 7.1 %all_gather.7 = bf16[768,256]{1,0:T(8,128)(2,1)S(1)} all-gather(bf16[192,256]{1,0:T(8,128)(2,1)S(1)} %copy-done.3), channel_id=1, replica_groups=mesh['mp'=8,'dp'=4] {'dp'}, dimensions={0}, use_global_device_ids=true | all-gather | bytes 491520 | tf_op jit(solution)/shard_map/all_gather | solution.py:53
  54.4 0.0 collective-permute-done
  54.4 0.0 collective-permute-done.1
  54.4 0.3 maximum_convert_fusion
  54.7 0.2 slice.54
  54.9 1.0 fusion.5
  55.9 0.1 slice.57
  56.1 0.8 fusion.11
  56.9 14.4 %all-gather.2.cloned.1.call-done = bf16[768,2048]{1,0:T(8,128)(2,1)} async-done(((bf16[192,2048]{1,0:T(8,128)(2,1)}), bf16[768,2048]{1,0:T(8,128)(2,1)}) %all-gather.2.cloned.1.call-update) | async-done | bytes 3145744 | tf_op jit(solution)/shard_map/all_gather | solution.py:56
  71.3 3.1 %fusion.13 = f32[192,768]{1,0:T(8,128)S(1)} fusion(bf16[192,2048]{0,1:T(8,128)(2,1)S(1)} %bitcast.10, bf16[768,2048]{1,0:T(8,128)(2,1)} %all-gather.2.cloned.1.call-done), kind=kOutput, calls=%fused_computation.31 | convolution fusion | flops 603979776 | bytes 4521984 | tf_op jit(solution)/shard_map/dot_general | solution.py:54
  74.4 1.1 fusion.14
  75.5 0.0 all-reduce.4.cloned.1.call-update
  75.5 0.0 reduce-scatter.2.cloned.1.call-start
  75.6 72.2 %all-reduce.4.cloned.1.call-done = f32[192,256]{1,0:T(8,128)} async-done(((f32[192,256]{1,0:T(8,128)}), f32[192,256]{1,0:T(8,128)}) %all-reduce.4.cloned.1.call-update) | async-done | bytes 196624 | tf_op jit(solution)/shard_map/psum | solution.py:63
  147.8 1.0 add_convert_fusion
  148.7 0.0 copy-start.2
  148.7 1.8 fusion.15
  150.5 0.0 reduce-scatter.2.cloned.1.call-update
  150.5 0.0 copy-done.2
  150.5 30.3 %reduce-scatter.2.cloned.1.call-done = f32[512,256]{1,0:T(8,128)} async-done(((f32[2048,256]{1,0:T(8,128)}), f32[512,256]{1,0:T(8,128)}) %reduce-scatter.2.cloned.1.call-update) | async-done | bytes 524304 | tf_op jit(solution)/shard_map/reduce_scatter | solution.py:65
  180.9 1.9 broadcast_multiply_fusion
  (4 shorter events, 0.0 us)
Async XLA Ops:
  7.2 2.3 %copy-start = (bf16[64,4,2048]{2,1,0:T(4,128)(2,1)S(1)}, bf16[64,4,2048]{2,1,0:T(4,128)(2,1)}, u32[]{:S(2)}) copy-start(bf16[64,4,2048]{2,1,0:T(4,128)(2,1)} %param.7) | copy-start | bytes 3145732
  7.2 64.1 %all-gather.2.cloned.1.call-start = ((), (), s32[]{:S(2)}) async-start(), calls=%async_computation.1 | async-start | bytes 3932160 | tf_op jit(solution)/shard_map/all_gather | solution.py:56
  9.5 9.6 %copy-start.1 = (bf16[16,4,2048]{2,1,0:T(4,128)(2,1)S(1)}, bf16[16,4,2048]{2,1,0:T(4,128)(2,1)}, u32[]{:S(2)}) copy-start(bf16[16,4,2048]{2,1,0:T(4,128)(2,1)} %param.6) | copy-start | bytes 786436
  38.5 8.8 %copy-start.3 = (bf16[192,256]{1,0:T(8,128)(2,1)S(1)}, bf16[192,256]{1,0:T(8,128)(2,1)}, u32[]{:S(2)}) copy-start(bf16[192,256]{1,0:T(8,128)(2,1)} %param.11) | copy-start | bytes 294916
  39.5 108.3 %all-reduce.4.cloned.1.call-start = ((), (), s32[]{:S(2)}) async-start(), calls=%async_computation.2 | async-start | bytes 393216 | tf_op jit(solution)/shard_map/psum | solution.py:63
  41.0 13.3 %collective-permute-start = (bf16[192,2,128]{0,2,1:T(8,128)(2,1)S(1)}, bf16[192,2,128]{0,2,1:T(8,128)(2,1)S(1)}, u32[]{:S(2)}, u32[]{:S(2)}) collective-permute-start(bf16[192,2,128]{0,2,1:T(8,128)(2,1)S(1)} %get-tuple-element.2), channel_id=1, source_target_pairs={{0,4},{4,8},{8,12},{12,16},{16,20},{20,24},{24,28},{1,5},{5,9},{9,... | collective-permute-start | bytes 294920 | tf_op jit(solution)/shard_map/ppermute | solution.py:18
  46.0 8.4 %collective-permute-start.1 = (bf16[192,2,128]{0,2,1:T(8,128)(2,1)S(1)}, bf16[192,2,128]{0,2,1:T(8,128)(2,1)S(1)}, u32[]{:S(2)}, u32[]{:S(2)}) collective-permute-start(bf16[192,2,128]{0,2,1:T(8,128)(2,1)S(1)} %get-tuple-element.3), channel_id=1, source_target_pairs={{4,0},{8,4},{12,8},{16,12},{20,16},{24,20},{28,24},{5,1},{9,5},{13... | collective-permute-start | bytes 294920 | tf_op jit(solution)/shard_map/ppermute | solution.py:19
  75.5 105.4 %reduce-scatter.2.cloned.1.call-start = ((), (), s32[]{:S(2)}) async-start(), calls=%async_computation.3 | async-start | bytes 2621440 | tf_op jit(solution)/shard_map/reduce_scatter | solution.py:65
  148.7 1.8 copy-start.2
Sparse Core Ops, SparseCore 0:
  39.6 31.6 all-gather.1
  75.7 72.0 all-reduce.3
  150.7 30.1 reduce-scatter.1
where the time goes:
time: 190 us; the launch traced here: 189 us
  waiting for transfers between devices  117 us (62%)
  local copies, waits for them, and re-layouts  21.9 us (12%)
  other arithmetic  17.1 us (9%)
  between operations  13.9 us (7%)
  blocking collectives  7.1 us (4%)
  starting transfers between devices  6.32 us (3%)
  matrix products  5.98 us (3%)
    psum x1, waiting for transfers between devices, per_device(): gram_prod = lax.psum(partial_value, 'mp') / (cells_here * slab_count)  72.2 us
    reduce_scatter x1, waiting for transfers between devices, per_device(): lax.psum_scatter(lax.dot_general(smooth, data_update, (((0,), (0,)), ((),...  30.3 us
    all_gather x1, waiting for transfers between devices, per_device(): lax.all_gather(sens, 'dp', axis=0, tiled=True)  14.4 us
    gather x1, local copies, waits for them, and re-layouts, per_device(): forward = forward_fields[data_freq].astype(jnp.float32)  9.69 us
    reduce_sum x1, other arithmetic, per_device(): jnp.sum(data_coef[:, :, None] * adjoint * forward, axis=1)  9.66 us
    gather x1, local copies, waits for them, and re-layouts, per_device(): adjoint = adjoint_fields[data_rec].astype(jnp.float32)  9.62 us
    all_gather x1, blocking collectives, per_device(): residual_whole = lax.all_gather(residual_cols, 'dp', axis=0, tiled=True)  7.1 us
    ppermute x1, starting transfers between devices, with_halo(): before = lax.ppermute(last, axis, up)  4.91 us
  transfers between devices with their start and end apart: 5, of which 3 were waited for; matrix products, arithmetic and copies ran while one was open for 2% of the time, Pallas kernels for 0%

commit v1 on v0

--- a/solution.py
+++ b/solution.py
@@ -6,6 +6,28 @@
 
 GRID_COLS = 128
 SWEEPS = 2
+
+
+def laid_out(parts, dim):
+    parts = jnp.moveaxis(parts, 0, dim)
+    dims = parts.shape
+    return parts.reshape(*dims[:dim], dims[dim] * dims[dim + 1], *dims[dim + 2 :])
+
+
+def grow_blocks(shard, axis):
+    size = lax.axis_size(axis)
+    tiles = shard[None]
+    for level in range(size.bit_length() - 1):
+        bit = 1 << level
+        theirs = lax.ppermute(tiles, axis, [(i, i ^ bit) for i in range(size)])
+        both = jnp.stack([tiles, theirs])
+        upper = lax.axis_index(axis) >> level & 1
+        tiles = jnp.where(upper == 0, both, both[::-1]).reshape(-1, *shard.shape)
+    return tiles
+
+
+def collect(array, axis, dim):
+    return laid_out(grow_blocks(array, axis), dim)
 
 
 def with_halo(array, sides, width):
@@ -52,10 +74,7 @@
     smooth = grid.reshape(rows_here, cells_here).astype(jnp.bfloat16)
     residual_whole = lax.all_gather(residual_cols, "dp", axis=0, tiled=True)
     gram_tile = lax.dot_general(
-        smooth,
-        lax.all_gather(sens, "dp", axis=0, tiled=True),
-        (((1,), (1,)), ((), ())),
-        preferred_element_type=jnp.float32,
+        smooth, collect(sens, "dp", 0), (((1,), (1,)), ((), ())), preferred_element_type=jnp.float32
     )
     partial_value = jnp.dot(
         gram_tile, residual_whole.astype(jnp.float32), precision=lax.Precision.HIGHEST

time: 190 us -> 208 us (1.095)
  blocking collectives: 7.1 us -> 32.4 us
  waiting for transfers between devices: 117 us -> 105 us
  other arithmetic: 17.1 us -> 22.2 us
    all_gather x1, blocking collectives: 7.1 us -> 32.4 us  [per_device(): residual_whole = lax.all_gather(residual_cols, 'dp', axis=0, tiled=True)]
    all_gather x1 -> x0, waiting for transfers between devices: 14.4 us -> none  [per_device(): lax.all_gather(sens, 'dp', axis=0, tiled=True)]
    another operation x0 -> x3, other arithmetic: none -> 3.99 us  [grow_blocks(): both = jnp.stack([tiles, theirs])]
    ppermute x0 -> x2, starting transfers between devices: none -> 3.33 us  [grow_blocks(): theirs = lax.ppermute(tiles, axis, [(i, i ^ bit) for i in range(size)])]
  transfers between devices with their start and end apart: 5 -> 6, of which waited for: 3 -> 3; matrix products, arithmetic and copies ran while one was open for 2% -> 2% of each run, Pallas kernels for 0% -> 0%
where the time goes in v1:
time: 208 us; the launch traced here: 207 us
  waiting for transfers between devices  105 us (50%)
  blocking collectives  32.4 us (16%)
  other arithmetic  22.2 us (11%)
  local copies, waits for them, and re-layouts  21.6 us (10%)
  between operations  14.2 us (7%)
  starting transfers between devices  8.14 us (4%)
  matrix products  4.09 us (2%)
    psum x1, waiting for transfers between devices, per_device(): gram_prod = lax.psum(partial_value, 'mp') / (cells_here * slab_count)  72.2 us
    all_gather x1, blocking collectives, per_device(): residual_whole = lax.all_gather(residual_cols, 'dp', axis=0, tiled=True)  32.4 us
    reduce_scatter x1, waiting for transfers between devices, per_device(): lax.psum_scatter(lax.dot_general(smooth, data_update, (((0,), (0,)), ((),...  30.3 us
    gather x1, local copies, waits for them, and re-layouts, per_device(): forward = forward_fields[data_freq].astype(jnp.float32)  9.69 us
    gather x1, local copies, waits for them, and re-layouts, per_device(): adjoint = adjoint_fields[data_rec].astype(jnp.float32)  9.61 us
    reduce_sum x1, other arithmetic, per_device(): jnp.sum(data_coef[:, :, None] * adjoint * forward, axis=1)  9.57 us
  transfers between devices with their start and end apart: 6, of which 3 were waited for; matrix products, arithmetic and copies ran while one was open for 2% of the time, Pallas kernels for 0%

profile of v1, /device:TPU:0, one launch (start us, length us, event | category | flops | bytes accessed | tf_op | source)
XLA Modules:
  0.0 207.3 jit_solution(18251442818615826535)
XLA Ops:
  7.2 0.0 copy-start
  7.2 0.0 all-reduce.4.cloned.1.call-start
  7.2 0.8 compare_select_fusion.1
  8.0 0.7 compare_select_fusion
  8.7 0.8 copy.10
  9.5 0.0 copy-done
  9.5 0.0 copy-start.1
  9.5 9.6 %gather_fusion = bf16[192,4,2048]{2,1,0:T(4,128)(2,1)} fusion(bf16[64,4,2048]{2,1,0:T(4,128)(2,1)S(1)} %copy-done, s32[1024]{0:T(1024)S(1)} %pad_clamp_fusion.1), kind=kCustom, calls=%fused_computation | custom fusion | bytes 6292224 | tf_op jit(solution)/shard_map/gather | solution.py:59
  19.1 0.0 copy-done.1
  19.1 9.7 %gather_fusion.1 = bf16[192,4,2048]{2,1,0:T(4,128)(2,1)} fusion(bf16[16,4,2048]{2,1,0:T(4,128)(2,1)S(1)} %copy-done.1, s32[1024]{0:T(1024)S(1)} %pad_clamp_fusion), kind=kCustom, calls=%fused_computation.1 | custom fusion | bytes 6292224 | tf_op jit(solution)/shard_map/gather | solution.py:60
  28.8 9.6 %multiply_reduce_fusion = f32[192,2048]{1,0:T(8,128)S(1)} fusion(bf16[192,4,2048]{2,1,0:T(4,128)(2,1)} %gather_fusion.1, bf16[192,4,2048]{2,1,0:T(4,128)(2,1)} %gather_fusion, f32[192,4]{1,0:T(8,128)S(1)} %copy.10), kind=kLoop, calls=%fused_computation.2 | loop fusion | flops 7471104 | bytes 7867392 | tf_op jit(solution)/shard_map/reduce_sum | solution.py:61
  38.4 1.0 fusion.25
  39.4 0.5 collective-permute-start.2
  39.9 0.1 fusion.24
  40.0 2.0 collective-permute-done.2
  42.0 0.1 pad_maximum_fusion.1
  42.2 2.2 %fusion.13 = (bf16[1,2,192,2048]{3,2,1,0:T(8,128)(2,1)}, bf16[2,192,2048]{2,1,0:T(8,128)(2,1)}) fusion(bf16[2,1,192,2048]{3,2,0,1:T(8,128)(2,1)S(1)} %pad_maximum_fusion.1, pred[]{:T(512)S(6)} %eq.7), kind=kLoop, calls=%fused_computation.28 | loop fusion | flops 786432 | bytes 4718593 | tf_op jit(solution)/shard_map/stack;reshape | solution.py:23
  44.3 0.0 copy-start.4
  44.3 2.9 %collective-permute-start.3 = (bf16[2,192,2048]{2,1,0:T(8,128)(2,1)}, bf16[2,192,2048]{2,1,0:T(8,128)(2,1)}, u32[]{:S(2)}, u32[]{:S(2)}) collective-permute-start(bf16[2,192,2048]{2,1,0:T(8,128)(2,1)} %get-tuple-element.3), channel_id=1, source_target_pairs={{0,2},{1,3},{2,0},{3,1},{4,6},{5,7},{6,4},{7,5},{8,10},{9,11},{10,... | collective-permute-start | bytes 4718600 | tf_op jit(solution)/shard_map/ppermute | solution.py:22
  47.2 0.1 multiply_convert_fusion
  47.3 0.5 copy.15
  47.8 3.4 %collective-permute-start = (bf16[192,2,128]{0,2,1:T(8,128)(2,1)S(1)}, bf16[192,2,128]{0,2,1:T(8,128)(2,1)S(1)}, u32[]{:S(2)}, u32[]{:S(2)}) collective-permute-start(bf16[192,2,128]{0,2,1:T(8,128)(2,1)S(1)} %get-tuple-element.4), channel_id=1, source_target_pairs={{0,4},{4,8},{8,12},{12,16},{16,20},{20,24},{24,28},{1,5},{5,9},{9,... | collective-permute-start | bytes 294920 | tf_op jit(solution)/shard_map/ppermute | solution.py:40
  51.3 1.3 collective-permute-start.1
  52.6 0.0 copy-done.4
  52.6 32.4 %all_gather.3 = bf16[768,256]{1,0:T(8,128)(2,1)S(1)} all-gather(bf16[192,256]{1,0:T(8,128)(2,1)S(1)} %copy-done.4), channel_id=1, replica_groups=mesh['mp'=8,'dp'=4] {'dp'}, dimensions={0}, use_global_device_ids=true | all-gather | bytes 491520 | tf_op jit(solution)/shard_map/all_gather | solution.py:75
  85.0 0.0 collective-permute-done
  85.0 0.0 collective-permute-done.1
  85.1 0.3 maximum_convert_fusion
  85.4 0.2 slice.54
  85.6 1.0 fusion.5
  86.6 0.2 slice.57
  86.8 0.0 copy-start.2
  86.8 0.8 fusion.11
  87.6 0.0 collective-permute-done.3
  87.6 0.6 copy-done.2
  88.2 1.7 pad_maximum_fusion
  89.9 0.9 reverse_select_fusion
  90.8 1.2 fusion.15
  92.0 1.1 fusion.16
  93.2 0.0 all-reduce.4.cloned.1.call-update
  93.2 0.0 reduce-scatter.2.cloned.1.call-start
  93.2 72.2 %all-reduce.4.cloned.1.call-done = f32[192,256]{1,0:T(8,128)} async-done(((f32[192,256]{1,0:T(8,128)}), f32[192,256]{1,0:T(8,128)}) %all-reduce.4.cloned.1.call-update) | async-done | bytes 196624 | tf_op jit(solution)/shard_map/psum | solution.py:82
  165.5 1.0 add_convert_fusion
  166.4 0.0 copy-start.3
  166.4 1.8 fusion.17
  168.2 0.0 reduce-scatter.2.cloned.1.call-update
  168.2 0.0 copy-done.3
  168.2 30.3 %reduce-scatter.2.cloned.1.call-done = f32[512,256]{1,0:T(8,128)} async-done(((f32[2048,256]{1,0:T(8,128)}), f32[512,256]{1,0:T(8,128)}) %reduce-scatter.2.cloned.1.call-update) | async-done | bytes 524304 | tf_op jit(solution)/shard_map/reduce_scatter | solution.py:84
  198.6 1.9 broadcast_multiply_fusion
  (4 shorter events, 0.0 us)
Async XLA Ops:
  7.2 2.3 %copy-start = (bf16[64,4,2048]{2,1,0:T(4,128)(2,1)S(1)}, bf16[64,4,2048]{2,1,0:T(4,128)(2,1)}, u32[]{:S(2)}) copy-start(bf16[64,4,2048]{2,1,0:T(4,128)(2,1)} %param.7) | copy-start | bytes 3145732
  7.2 158.3 %all-reduce.4.cloned.1.call-start = ((), (), s32[]{:S(2)}) async-start(), calls=%async_computation.1 | async-start | bytes 393216 | tf_op jit(solution)/shard_map/psum | solution.py:82
  9.5 9.6 %copy-start.1 = (bf16[16,4,2048]{2,1,0:T(4,128)(2,1)S(1)}, bf16[16,4,2048]{2,1,0:T(4,128)(2,1)}, u32[]{:S(2)}) copy-start(bf16[16,4,2048]{2,1,0:T(4,128)(2,1)} %param.6) | copy-start | bytes 786436
  39.4 2.6 %collective-permute-start.2 = (bf16[1,192,2048]{2,1,0:T(8,128)(2,1)}, bf16[1,192,2048]{2,1,0:T(8,128)(2,1)S(1)}, u32[]{:S(2)}, u32[]{:S(2)}) collective-permute-start(bf16[1,192,2048]{2,1,0:T(8,128)(2,1)} %fusion.25), channel_id=1, source_target_pairs={{0,1},{1,0},{2,3},{3,2},{4,5},{5,4},{6,7},{7,6},{8,9},{9,8},{10,11... | collective-permute-start | bytes 2359304 | tf_op jit(solution)/shard_map/ppermute | solution.py:22
  44.3 8.3 %copy-start.4 = (bf16[192,256]{1,0:T(8,128)(2,1)S(1)}, bf16[192,256]{1,0:T(8,128)(2,1)}, u32[]{:S(2)}) copy-start(bf16[192,256]{1,0:T(8,128)(2,1)} %param.11) | copy-start | bytes 294916
  44.3 43.3 %collective-permute-start.3 = (bf16[2,192,2048]{2,1,0:T(8,128)(2,1)}, bf16[2,192,2048]{2,1,0:T(8,128)(2,1)}, u32[]{:S(2)}, u32[]{:S(2)}) collective-permute-start(bf16[2,192,2048]{2,1,0:T(8,128)(2,1)} %get-tuple-element.3), channel_id=1, source_target_pairs={{0,2},{1,3},{2,0},{3,1},{4,6},{5,7},{6,4},{7,5},{8,10},{9,11},{10,... | collective-permute-start | bytes 4718600 | tf_op jit(solution)/shard_map/ppermute | solution.py:22
  47.8 37.2 %collective-permute-start = (bf16[192,2,128]{0,2,1:T(8,128)(2,1)S(1)}, bf16[192,2,128]{0,2,1:T(8,128)(2,1)S(1)}, u32[]{:S(2)}, u32[]{:S(2)}) collective-permute-start(bf16[192,2,128]{0,2,1:T(8,128)(2,1)S(1)} %get-tuple-element.4), channel_id=1, source_target_pairs={{0,4},{4,8},{8,12},{12,16},{16,20},{20,24},{24,28},{1,5},{5,9},{9,... | collective-permute-start | bytes 294920 | tf_op jit(solution)/shard_map/ppermute | solution.py:40
  51.3 33.8 %collective-permute-start.1 = (bf16[192,2,128]{0,2,1:T(8,128)(2,1)S(1)}, bf16[192,2,128]{0,2,1:T(8,128)(2,1)S(1)}, u32[]{:S(2)}, u32[]{:S(2)}) collective-permute-start(bf16[192,2,128]{0,2,1:T(8,128)(2,1)S(1)} %get-tuple-element.5), channel_id=1, source_target_pairs={{4,0},{8,4},{12,8},{16,12},{20,16},{24,20},{28,24},{5,1},{9,5},{13... | collective-permute-start | bytes 294920 | tf_op jit(solution)/shard_map/ppermute | solution.py:41
  86.8 1.4 copy-start.2
  93.2 105.4 %reduce-scatter.2.cloned.1.call-start = ((), (), s32[]{:S(2)}) async-start(), calls=%async_computation.2 | async-start | bytes 2621440 | tf_op jit(solution)/shard_map/reduce_scatter | solution.py:84
  166.4 1.8 copy-start.3
Sparse Core Ops, SparseCore 0:
  93.3 72.1 all-reduce.3
  168.4 30.1 reduce-scatter.1
